TPU v7x, 512 devices: a whole 4x4x16 slice. The times are simulated.
512 devices in a mesh: seq: 128 (over x, z, core), batch: 4 (over y).
Axes of the slice: x: 4, y: 4, z: 16, core: 2. Of those that a mesh axis runs over, the one named last changes fastest.
Arguments:
- dna_bases: int32 [131072], P(('batch', 'seq')), parts along dimension 0, may hold values from 0 to 3
- stem_weight: bfloat16 [5, 4, 384], replicated, may hold values from -8 to 8
- stem_bias: float32 [384], replicated, may hold values from -4 to 0
- conv_weight: bfloat16 [5, 384, 768], replicated, may hold values from -0.4375 to 0.4375
- conv_bias: float32 [768], replicated, may hold values from -4 to 0
- norm_gain: float32 [768], replicated, may hold values from 0.25 to 1.75
- query_weight: bfloat16 [768, 1024], replicated, may hold values from -0.875 to 0.875
- key_weight: bfloat16 [768, 128], replicated, may hold values from -0.21875 to 0.21875
- value_weight: bfloat16 [768, 192], replicated, may hold values from -0.4375 to 0.4375
Outputs:
- attended: bfloat16 [32768, 1536], P(('batch', 'seq')), parts along dimension 0
There are 4 independent parts, one for each index of `batch`. A program takes and returns all parts, laid end to end along the dimension named above; an argument that names none is the same for every part. Nothing has to cross between parts.
Inputs may be any that keep to these rules, and one draw needn't show every extreme that they name: `dna_bases`: codes for A, C, G and T in this order.
All inputs are finite; a program needn't handle non-finite values.
Results may differ from a plain program's by a relative error of at most 0.005.
Values may be sent and summed in bfloat16 or wider, within the bound.
A program may use at most 64 MiB of HBM per device.

v0:
```python
import math

import jax
import jax.numpy as jnp
from jax import lax
from jax.sharding import PartitionSpec as P

soft_cap = 20.0
rope_base = 10000.0


def padded_2(x, sides, width):
    for axis, dim in sides:
        peers, length = (lax.axis_size(axis), x.shape[dim])
        up = [(i, (i + 1) % peers) for i in range(peers - 1)]
        down = [(j, i) for i, j in up]
        last = lax.slice_in_dim(x, length - width, length, axis=dim)
        initial = lax.slice_in_dim(x, 0, width, axis=dim)
        before = lax.ppermute(last, axis, up)
        after = lax.ppermute(initial, axis, down)
        x = jnp.concatenate([before, x, after], axis=dim)
    return x


def encode(base_marks):
    return (base_marks[:, None] == jnp.arange(1, 5, dtype=jnp.int32)[None, :]).astype(jnp.bfloat16)


def shifted_sum(inputs, weight, shift_bias):
    out_rows = inputs.shape[0] - weight.shape[0] + 1
    summed = jnp.zeros((out_rows, weight.shape[2]), jnp.float32) + shift_bias[None, :]
    for offset in range(weight.shape[0]):
        summed = summed + jnp.dot(
            inputs[offset : offset + out_rows], weight[offset], preferred_element_type=jnp.float32
        )
    return summed


def gelu_pool(values_in):
    activated = jax.nn.gelu(values_in, approximate=True)
    return activated.reshape(values_in.shape[0] // 2, 2, values_in.shape[1]).max(axis=1)


def normalize(features, norm_gain):
    mean_square = jnp.mean(features * features, axis=1, keepdims=True)
    return (features * lax.rsqrt(mean_square + 1e-06) * norm_gain[None, :]).astype(jnp.bfloat16)


def rotate(vectors, places):
    half_size = vectors.shape[-1] // 2
    frequency = jnp.exp(
        jnp.arange(half_size, dtype=jnp.float32) * (-2.0 * math.log(rope_base) / vectors.shape[-1])
    )
    angles = places.astype(jnp.float32)[:, None] * frequency[None, :]
    cosine = jnp.cos(angles)[:, None, :]
    sine_part = jnp.sin(angles)[:, None, :]
    first_half = vectors[..., :half_size]
    second_half = vectors[..., half_size:]
    return jnp.concatenate(
        [
            first_half * cosine - second_half * sine_part,
            second_half * cosine + first_half * sine_part,
        ],
        axis=-1,
    )


def accumulate(queries, key_piece, value_piece, score_scale):
    raw_scores = (
        jnp.einsum("qhd,kd->qhk", queries, key_piece, preferred_element_type=jnp.float32)
        * score_scale
    )
    capped = soft_cap * jnp.tanh(raw_scores / soft_cap)
    probability = jnp.exp(capped - soft_cap)
    totals = jnp.sum(probability, axis=2)
    weighted = jnp.einsum(
        "qhk,kv->qhv",
        probability.astype(jnp.bfloat16),
        value_piece,
        preferred_element_type=jnp.float32,
    )
    return (weighted, totals)


def on_device(
    dna_bases,
    stem_weight,
    stem_bias,
    conv_weight,
    conv_bias,
    norm_gain,
    query_weight,
    key_weight,
    value_weight,
):
    position = lax.axis_index("seq")
    base_marks = dna_bases + 1
    stem_reach = stem_weight.shape[0] // 2
    conv_reach = conv_weight.shape[0] // 2
    extended = padded_2(base_marks, (("seq", 0),), stem_reach)
    pooled = gelu_pool(shifted_sum(encode(extended), stem_weight, stem_bias)).astype(jnp.bfloat16)
    padded = padded_2(pooled, (("seq", 0),), conv_reach)
    features = gelu_pool(shifted_sum(padded, conv_weight, conv_bias))
    normed = normalize(features, norm_gain)
    token_rows = normed.shape[0]
    key_size = key_weight.shape[1]
    value_size = value_weight.shape[1]
    head_count = query_weight.shape[1] // key_size
    places = position * token_rows + jnp.arange(token_rows, dtype=jnp.int32)
    queries = rotate(
        jnp.dot(normed, query_weight, preferred_element_type=jnp.float32).reshape(
            token_rows, head_count, key_size
        ),
        places,
    ).astype(jnp.bfloat16)
    key_rows = rotate(
        jnp.dot(normed, key_weight, preferred_element_type=jnp.float32)[:, None, :], places
    )[:, 0, :].astype(jnp.bfloat16)
    value_rows = jnp.dot(normed, value_weight, preferred_element_type=jnp.float32).astype(
        jnp.bfloat16
    )
    score_scale = 1.0 / math.sqrt(key_size)
    weighted, totals = accumulate(
        queries,
        lax.all_gather(key_rows, "seq", axis=0, tiled=True),
        lax.all_gather(value_rows, "seq", axis=0, tiled=True),
        score_scale,
    )
    return (
        (weighted / totals[:, :, None])
        .astype(jnp.bfloat16)
        .reshape(token_rows, head_count * value_size)
    )


def solution(mesh):
    placed = (P(("batch", "seq")), P(), P(), P(), P(), P(), P(), P(), P())
    return jax.shard_map(
        on_device, mesh=mesh, in_specs=placed, out_specs=P(("batch", "seq"), None), check_vma=False
    )
```

profile of v0, /device:TPU:1, one launch (start us, length us, event | category | flops | bytes accessed | tf_op | source)
XLA Modules:
  0.0 338.4 jit_solution(12866878667711757721)
XLA Ops:
  6.5 0.8 broadcast_add_fusion
  7.3 0.1 fusion.84
  7.4 4.9 %collective-permute-start = (s32[2]{0:T(128)S(1)}, s32[2]{0:T(128)S(1)}, u32[]{:S(2)}, u32[]{:S(2)}) collective-permute-start(s32[2]{0:T(128)S(1)} %get-tuple-element.13), channel_id=1, source_target_pairs={{0,4},{4,8},{8,12},{12,16},{16,20},{20,24},{24,28},{28,32},{32,36}... | collective-permute-start | bytes 32 | tf_op jit(solution)/shard_map/ppermute | solution.py:19
  12.3 5.1 %collective-permute-start.1 = (s32[2]{0:T(128)S(1)}, s32[2]{0:T(128)S(1)}, u32[]{:S(2)}, u32[]{:S(2)}) collective-permute-start(s32[2]{0:T(128)S(1)} %get-tuple-element.14), channel_id=1, source_target_pairs={{4,0},{8,4},{12,8},{16,12},{20,16},{24,20},{28,24},{32,28},{36,32}... | collective-permute-start | bytes 32 | tf_op jit(solution)/shard_map/ppermute | solution.py:20
  17.5 0.0 collective-permute-done
  17.6 0.7 collective-permute-done.1
  18.3 0.1 pad_add_fusion
  18.4 0.1 broadcast_compare_fusion
  18.5 0.9 convolution_add_fusion.6
  19.4 0.9 convolution_add_fusion.5
  20.3 0.9 convolution_add_fusion.4
  21.1 0.0 copy-start.3
  21.1 0.9 convolution_add_fusion.3
  22.0 1.0 fusion.36
  23.0 0.1 reshape.133
  23.1 0.5 reduce_max.18
  23.6 1.9 collective-permute-start.2
  25.5 1.3 fusion.20
  26.9 2.4 collective-permute-start.3
  29.3 0.0 collective-permute-done.2
  29.3 1.3 fusion.22
  30.6 1.1 collective-permute-done.3
  31.8 1.3 fusion.17
  33.1 0.0 copy-start.4
  33.1 0.0 copy-start.2
  33.1 0.0 copy-start.1
  33.1 1.4 fusion.5
  34.5 1.4 fusion.43
  35.9 0.2 reshape.134
  36.2 0.5 reduce_max.19
  36.6 0.1 multiply_reduce_fusion
  36.8 0.1 multiply_convert_fusion
  36.9 0.2 convolution_bitcast_fusion.1
  37.1 0.2 fusion.65
  37.3 0.7 pad_maximum_fusion.4
  37.9 0.0 all-gather.6.cloned.1.call-update
  38.0 0.0 all-gather.4.cloned.1.call-start
  38.0 0.0 copy-done.1
  38.0 0.9 convolution_convert_fusion
  38.9 0.0 all-gather.4.cloned.1.call-update
  38.9 0.2 multiply_cosine_fusion.1
  39.1 0.4 convolution_bitcast_fusion
  39.6 0.2 subtract_convert_fusion
  39.7 142.6 %all-gather.6.cloned.1.call-done = bf16[8192,1,128]{2,0,1:T(8,128)(2,1)} async-done(((bf16[64,1,128]{2,0,1:T(8,128)(2,1)}), bf16[8192,1,128]{2,0,1:T(8,128)(2,1)}) %all-gather.6.cloned.1.call-update) | async-done | bytes 2097168 | tf_op jit(solution)/shard_map/all_gather | solution.py:125
  182.3 9.2 %fusion.85 = (f32[64,8]{1,0:T(8,128)S(1)}, bf16[64,8,8192]{2,1,0:T(8,128)(2,1)}) fusion(bf16[8192,1,128]{2,0,1:T(8,128)(2,1)} %all-gather.6.cloned.1.call-done, bf16[64,8,64]{2,1,0:T(8,128)(2,1)S(1)} %get-tuple-element.6, bf16[64,8,64]{2,1,0:T(8,128)(2,1)S(1)} %get-tuple-element.5), kind=kOutput, calls=%fused_computation.108 | convolution fusion | flops 1094974976 | bytes 10618880 | tf_op jit(solution)/shard_map/qhd,kd->qhk/dot_general | solution.py:70
  191.5 132.2 %all-gather.4.cloned.1.call-done = bf16[8192,192]{1,0:T(8,128)(2,1)} async-done(((bf16[64,192]{1,0:T(8,128)(2,1)}), bf16[8192,192]{1,0:T(8,128)(2,1)}) %all-gather.4.cloned.1.call-update) | async-done | bytes 3145744 | tf_op jit(solution)/shard_map/all_gather | solution.py:126
  323.7 6.9 %fusion.12 = bf16[64,8,192]{2,1,0:T(8,128)(2,1)S(1)} fusion(bf16[8192,192]{1,0:T(8,128)(2,1)} %all-gather.4.cloned.1.call-done, bf16[64,8,8192]{2,1,0:T(8,128)(2,1)} %get-tuple-element.16, f32[64,8]{1,0:T(8,128)S(1)} %get-tuple-element.15), kind=kOutput, calls=%fused_computation.16 | convolution fusion | flops 1610809344 | bytes 11732992 | tf_op jit(solution)/shard_map/qhk,kv->qhv/dot_general | solution.py:76
  330.6 0.9 reshape.136
  (12 shorter events, 0.1 us)
Async XLA Ops:
  6.5 32.6 %copy-start = (bf16[768,1024]{1,0:T(8,128)(2,1)S(1)}, bf16[768,1024]{1,0:T(8,128)(2,1)}, u32[]{:S(2)}) copy-start(bf16[768,1024]{1,0:T(8,128)(2,1)} %param.15) | copy-start | bytes 4718596
  6.5 175.8 %all-gather.6.cloned.1.call-start = ((), (), s32[]{:S(2)}) async-start(), calls=%async_computation.1 | async-start | bytes 2113536 | tf_op jit(solution)/shard_map/all_gather | solution.py:125
  7.4 10.1 %collective-permute-start = (s32[2]{0:T(128)S(1)}, s32[2]{0:T(128)S(1)}, u32[]{:S(2)}, u32[]{:S(2)}) collective-permute-start(s32[2]{0:T(128)S(1)} %get-tuple-element.13), channel_id=1, source_target_pairs={{0,4},{4,8},{8,12},{12,16},{16,20},{20,24},{24,28},{28,32},{32,36}... | collective-permute-start | bytes 32 | tf_op jit(solution)/shard_map/ppermute | solution.py:19
  12.3 5.9 %collective-permute-start.1 = (s32[2]{0:T(128)S(1)}, s32[2]{0:T(128)S(1)}, u32[]{:S(2)}, u32[]{:S(2)}) collective-permute-start(s32[2]{0:T(128)S(1)} %get-tuple-element.14), channel_id=1, source_target_pairs={{4,0},{8,4},{12,8},{16,12},{20,16},{24,20},{28,24},{32,28},{36,32}... | collective-permute-start | bytes 32 | tf_op jit(solution)/shard_map/ppermute | solution.py:20
  21.1 12.0 %copy-start.3 = (f32[768]{0:T(1024)S(1)}, f32[768]{0:T(1024)}, u32[]{:S(2)}) copy-start(f32[768]{0:T(1024)} %param.13) | copy-start | bytes 9220
  23.6 5.7 %collective-permute-start.2 = (bf16[2,384]{1,0:T(2,128)(2,1)S(1)}, bf16[2,384]{1,0:T(2,128)(2,1)S(1)}, u32[]{:S(2)}, u32[]{:S(2)}) collective-permute-start(bf16[2,384]{1,0:T(2,128)(2,1)S(1)} %get-tuple-element.7), channel_id=1, source_target_pairs={{0,4},{4,8},{8,12},{12,16},{16,20},{20,24},{24,28},{28,32},{32,36}... | collective-permute-start | bytes 4616 | tf_op jit(solution)/shard_map/ppermute | solution.py:19
  26.9 4.9 %collective-permute-start.3 = (bf16[2,384]{1,0:T(2,128)(2,1)S(1)}, bf16[2,384]{1,0:T(2,128)(2,1)S(1)}, u32[]{:S(2)}, u32[]{:S(2)}) collective-permute-start(bf16[2,384]{1,0:T(2,128)(2,1)S(1)} %get-tuple-element.8), channel_id=1, source_target_pairs={{4,0},{8,4},{12,8},{16,12},{20,16},{24,20},{28,24},{32,28},{36,32}... | collective-permute-start | bytes 4616 | tf_op jit(solution)/shard_map/ppermute | solution.py:20
  33.1 3.7 %copy-start.4 = (f32[768]{0:T(1024)S(1)}, f32[768]{0:T(1024)}, u32[]{:S(2)}) copy-start(f32[768]{0:T(1024)} %param.14) | copy-start | bytes 9220
  33.1 3.8 %copy-start.2 = (bf16[768,128]{1,0:T(8,128)(2,1)S(1)}, bf16[768,128]{1,0:T(8,128)(2,1)}, u32[]{:S(2)}) copy-start(bf16[768,128]{1,0:T(8,128)(2,1)} %param.16) | copy-start | bytes 589828
  33.1 4.9 %copy-start.1 = (bf16[768,192]{0,1:T(8,128)(2,1)S(1)}, bf16[768,192]{0,1:T(8,128)(2,1)}, u32[]{:S(2)}) copy-start(bf16[768,192]{0,1:T(8,128)(2,1)} %param.17) | copy-start | bytes 884740
  38.0 285.8 %all-gather.4.cloned.1.call-start = ((), (), s32[]{:S(2)}) async-start(), calls=%async_computation | async-start | bytes 4227072 | tf_op jit(solution)/shard_map/all_gather | solution.py:126
Sparse Core Ops, SparseCore 0:
  38.1 144.1 all-gather.5
  185.5 138.2 all-gather.3
where the time goes:
time: 339 us; the launch traced here: 338 us
  waiting for transfers between devices  277 us (82%)
  matrix products  28.7 us (8%)
  starting transfers between devices  14.4 us (4%)
  between operations  13.7 us (4%)
  other arithmetic  3.42 us (1%)
    all_gather x1, waiting for transfers between devices, on_device(): lax.all_gather(key_rows, 'seq', axis=0, tiled=True)  143 us
    all_gather x1, waiting for transfers between devices, on_device(): lax.all_gather(value_rows, 'seq', axis=0, tiled=True)  132 us
    dot_general x10, matrix products, shifted_sum(): jnp.dot(inputs[offset:offset + out_rows], weight[offset], preferred_eleme...  11.2 us
    dot_general x1, matrix products, accumulate(): jnp.einsum('qhd,kd->qhk', queries, key_piece, preferred_element_type=jnp....  9.2 us
    ppermute x2, starting transfers between devices, padded_2(): after = lax.ppermute(initial, axis, down)  7.54 us
    dot_general x1, matrix products, accumulate(): jnp.einsum('qhk,kv->qhv', probability.astype(jnp.bfloat16), value_piece,...  6.9 us
    ppermute x2, starting transfers between devices, padded_2(): before = lax.ppermute(last, axis, up)  6.84 us
  transfers between devices with their start and end apart: 6, of which 4 were waited for; matrix products, arithmetic and copies ran while one was open for 4% of the time, Pallas kernels for 0%

commit v1 on v0

v1 whole, which is shorter than its diff:
```python
import functools
import math

import jax
import jax.numpy as jnp
import numpy as np
from jax import lax
from jax.experimental import pallas as pl
from jax.experimental.pallas import tpu as pltpu
from jax.sharding import PartitionSpec as P

MESH = pl.DeviceIdType.MESH
SOFT_CAP = 20.0
ROPE_BASE = 10000.0
NX, NZ = 4, 16
TOK = 64
C1, C2, HEADS, KD, VD, TAPS = 384, 768, 8, 128, 192, 5
UROWS = 80
QROWS = TOK * HEADS
F32, BF16 = jnp.float32, jnp.bfloat16

U_C, U_R2, U_R1, U_L1, U_L2, U_O = 0, 2, 3, 4, 5, 6


def chunk(direction, step):
    if step == 0:
        return 0
    if step == 8:
        return 15
    return step if direction == 0 else 7 + step


def gelu(x):
    inner = math.sqrt(2.0 / math.pi) * (x + 0.044715 * (x * x * x))
    return (0.5 * x) * (1.0 + jnp.tanh(inner))


class Copies:
    def __init__(self, send, recv):
        self.send, self.recv, self.made = send, recv, []

    def start(self, src, dst, to):
        k = len(self.made)
        copy = pltpu.make_async_remote_copy(
            src_ref=src, dst_ref=dst, send_sem=self.send.at[k], recv_sem=self.recv.at[k],
            device_id={"seq": to}, device_id_type=MESH,
        )
        copy.start()
        self.made.append(copy)
        return copy


N_COPIES = 96


def kernel(
    bases_ref, stem_w_ref, stem_b_ref, conv_b_ref, gain_ref, rope_ref, step_ref,
    conv_w_hbm, query_w_hbm, key_w_hbm, value_w_hbm,
    out_ref,
    halo, onehot, stem_w, pooled_e, pooled_o, conv_in, conv_w, query_w, key_w, value_w,
    buf, q_buf, acc, tot, part, send, recv, load,
):
    me = lax.axis_index("seq")
    core, z, x = me % 2, (me // 2) % NZ, me // (2 * NZ)

    def at(xx, zz, cc):
        return ((xx % NX) * NZ + zz % NZ) * 2 + cc

    x_up, x_down = at(x + 1, z, core), at(x + NX - 1, z, core)
    z_up, z_down = at(x, z + 1, core), at(x, z + NZ - 1, core)
    twin = at(x, z, 1 - core)
    after, before = (me + 1) % (2 * NX * NZ), (me + 2 * NX * NZ - 1) % (2 * NX * NZ)
    other = jnp.where(core == 0, before, after)

    loads = [
        pltpu.make_async_copy(conv_w_hbm, conv_w, load.at[0]),
        pltpu.make_async_copy(key_w_hbm, key_w, load.at[1]),
        pltpu.make_async_copy(value_w_hbm, value_w.at[pl.ds(0, VD)], load.at[2]),
        pltpu.make_async_copy(value_w_hbm.at[pl.ds(KD, VD - KD)], value_w.at[pl.ds(VD, VD - KD)], load.at[3]),
        pltpu.make_async_copy(query_w_hbm, query_w, load.at[4]),
    ]
    for one in loads:
        one.start()

    barrier = pltpu.get_barrier_semaphore()
    for peer in (x_up, x_down, z_up, z_down, twin, other):
        pl.semaphore_signal(barrier, inc=1, device_id={"seq": peer}, device_id_type=MESH)
    pl.semaphore_wait(barrier, 6)

    copies = Copies(send, recv)
    from_before = copies.start(bases_ref, halo.at[0], after)
    from_after = copies.start(bases_ref, halo.at[1], before)

    stem_w[...] = jnp.zeros_like(stem_w)
    for t in range(TAPS):
        stem_w[t * 8 : t * 8 + 4, :] = stem_w_ref[t].astype(F32)
    dev = step_ref[pl.ds(me, 1), :]
    cos_d, sin_d = dev[:, :KD], dev[:, KD:]
    cos_r, sin_r = rope_ref[:, :KD], rope_ref[:, KD:]
    lane = lax.broadcasted_iota(jnp.int32, (TOK, KD), 1)
    cos = cos_d * cos_r - sin_d * sin_r
    sin = sin_d * cos_r + cos_d * sin_r
    sin = jnp.where(lane < KD // 2, -sin, sin)

    def rotate(u):
        return u * cos + pltpu.roll(u, KD // 2, 1) * sin

    from_before.wait_recv()
    from_after.wait_recv()

    lanes = lax.broadcasted_iota(jnp.int32, (8, 128), 1)
    left = jnp.where(me == 0, 0, pltpu.roll(halo[0], 66, 1))
    right = jnp.where(me == 2 * NX * NZ - 1, 0, pltpu.roll(halo[1], 66, 1))
    own = pltpu.roll(bases_ref[...], 2, 1)
    marks = jnp.where(lanes < 2, left, jnp.where(lanes < 66, own, jnp.where(lanes < 68, right, 0)))
    moved = [marks, pltpu.roll(marks, 127, 1), pltpu.roll(marks, 126, 1)]
    base = lax.broadcasted_iota(jnp.int32, (8, 128), 0) + 1
    for r in range(4):
        for t in range(TAPS):
            k = r + t - 2
            row = moved[1 + k // 4][k % 4 : k % 4 + 1, :]
            onehot[t * 8 : t * 8 + 8, r * 128 : (r + 1) * 128] = (
                jnp.broadcast_to(row, (8, 128)) == base
            ).astype(F32)
    stem = lax.dot_general(
        onehot[...].astype(BF16), stem_w[...].astype(BF16), (((0,), (0,)), ((), ())),
        preferred_element_type=F32,
    )
    stem = [gelu(stem[r * 128 : r * 128 + 72] + stem_b_ref[...]) for r in range(4)]
    spot = lax.broadcasted_iota(jnp.int32, (72, C1), 0)
    first = jnp.where(me == 0, 1, 0)
    last = jnp.where(me == 2 * NX * NZ - 1, 64, 65)
    inside = (spot >= first) & (spot <= last)
    pooled_e[...] = jnp.where(inside, jnp.maximum(stem[0], stem[1]), 0.0)
    pooled_o[...] = jnp.where(inside, jnp.maximum(stem[2], stem[3]), 0.0)

    shifted = [[ref[pl.ds(o, TOK), :].astype(BF16) for ref in (pooled_e, pooled_o)] for o in range(3)]
    for t in range(TAPS):
        conv_in[0:TOK, t * C1 : (t + 1) * C1] = shifted[t // 2][t % 2]
        conv_in[TOK : 2 * TOK, t * C1 : (t + 1) * C1] = shifted[(t + 1) // 2][(t + 1) % 2]
    loads[0].wait()
    conv = jnp.dot(
        conv_in[...], conv_w[...].reshape(TAPS * C1, C2), preferred_element_type=F32
    ) + conv_b_ref[...]
    conv = gelu(conv)
    features = jnp.maximum(conv[:TOK], conv[TOK:])
    mean_square = jnp.mean(features * features, axis=1, keepdims=True)
    normed = (features * lax.rsqrt(mean_square + 1e-06) * gain_ref[...]).astype(BF16)

    for one in loads[1:4]:
        one.wait()
    keys = rotate(jnp.dot(normed, key_w[...], preferred_element_type=F32)).astype(BF16)
    values = lax.dot_general(normed, value_w[...], (((1,), (1,)), ((), ())), preferred_element_type=F32)
    tails = values[:, KD:]
    values = values[:, :KD].astype(BF16)
    half = lax.broadcasted_iota(jnp.int32, (16, KD), 1) < KD // 2
    for u in range(2):
        buf[0, u, 0:32, :] = keys[u * 32 : u * 32 + 32]
        buf[0, u, 32:64, :] = values[u * 32 : u * 32 + 32]
        buf[0, u, 64:80, :] = jnp.where(
            half, tails[u * 32 : u * 32 + 16], tails[u * 32 + 16 : u * 32 + 32]
        ).astype(BF16)

    def units(c, u, n=1):
        return buf.at[c, pl.ds(u, n)]

    z_to = (z_up, z_down)
    arrive_a, arrive_b, arrive_x, arrive_o = {}, {}, {}, {}

    def send_a(direction, step):
        if step < 7 or (step == 7 and direction == 0):
            src, dst = chunk(direction, step), chunk(direction, step + 1)
            arrive_a[dst] = copies.start(units(src, U_C, 2), units(dst, U_C, 2), z_to[direction])

    def send_b(direction, step):
        if step < 7 or (step == 7 and direction == 1):
            src, dst = chunk(direction, step), chunk(direction, step + 1)
            arrive_b[dst] = copies.start(units(src, U_R1, 2), units(dst, U_R1, 2), z_to[direction])

    def send_x(c):
        arrive_x[c] = (
            copies.start(units(c, U_C + 1), units(c, U_L2), x_up),
            copies.start(units(c, U_C + 1), units(c, U_R2), x_down),
        )

    def send_o(c):
        if c in (0, 15):
            arrive_o[c] = (
                copies.start(units(c, U_L1), units(c, U_O), x_up),
                copies.start(units(c, U_R2), units(c, U_O + 1), x_down),
            )
        elif c < 8:
            arrive_o[c] = (copies.start(units(c, U_L1, 2), units(c, U_O, 2), x_up),)
        else:
            arrive_o[c] = (copies.start(units(c, U_R2, 2), units(c, U_O, 2), x_down),)

    arrive_b[0] = (
        copies.start(units(0, U_C), units(0, U_L1), x_up),
        copies.start(units(0, U_C), units(0, U_R1), x_down),
    )
    send_a(0, 0)
    send_a(1, 0)
    send_x(0)

    loads[4].wait()
    for h in range(HEADS):
        u = jnp.dot(normed, query_w[:, h * KD : (h + 1) * KD], preferred_element_type=F32)
        q_buf[0, h * TOK : (h + 1) * TOK, :] = rotate(u).astype(BF16)
        if h == 3:
            for copy in arrive_b[0]:
                copy.wait_recv()
            send_b(0, 0)
            send_b(1, 0)
    queries = copies.start(q_buf.at[0], q_buf.at[1], twin)
    for copy in arrive_x[0]:
        copy.wait_recv()
    send_o(0)

    acc[...] = jnp.zeros_like(acc)
    tot[...] = jnp.zeros_like(tot)

    scale = 1.0 / math.sqrt(KD) / SOFT_CAP
    peak = SOFT_CAP * math.log2(math.e)
    rows = 256

    def attend(c, owner):
        key_rows = buf[c, :, 0:32, :].reshape(256, KD)
        value_rows = buf[c, :, 32:64, :].reshape(256, KD)
        tail = buf[c, :, 64:80, :]
        turned = pltpu.roll(tail.astype(F32).reshape(128, KD), KD // 2, 1).astype(BF16).reshape(8, 16, KD)
        tail = jnp.concatenate([tail, turned], axis=1).reshape(256, KD)
        right_side = jnp.concatenate([value_rows, tail], axis=1)

        def body(i, carry):
            at_rows = pl.ds(pl.multiple_of(i * rows, rows), rows)
            scores = lax.dot_general(
                q_buf[owner, at_rows, :], key_rows, (((1,), (1,)), ((), ())), preferred_element_type=F32
            )
            probability = jnp.exp2(jnp.tanh(scores * scale) * peak - peak)
            tot[owner, at_rows, :] += probability[:, :128] + probability[:, 128:]
            acc[owner, at_rows, :] += jnp.dot(
                probability.astype(BF16), right_side, preferred_element_type=F32
            )
            return carry

        lax.fori_loop(0, QROWS // rows, body, 0)

    def complete(c):
        for copy in arrive_o[c]:
            copy.wait_recv()

    queries.wait_recv()
    for step in range(1, 9):
        pair = (chunk(0, step), chunk(1, step)) if step < 8 else (15,)
        ready = [] if step == 2 else [0] if step == 1 else [chunk(0, step - 2), chunk(1, step - 2)]
        for c in pair:
            direction = 0 if c < 8 or c == 15 else 1
            arrive_a[c].wait_recv()
            send_a(direction, step)
            send_x(c)
        if ready:
            complete(ready[0])
            attend(ready[0], 1)
        for c in pair:
            direction = 0 if c < 8 else 1
            arrive_b[c].wait_recv()
            send_b(direction, step)
        if ready:
            attend(ready[0], 0)
        if step > 1:
            for direction in (0, 1):
                c = chunk(direction, step - 1)
                for copy in arrive_x[c]:
                    copy.wait_recv()
                send_o(c)
        if len(ready) > 1:
            complete(ready[1])
            attend(ready[1], 1)
            attend(ready[1], 0)
    for copy in arrive_x[15]:
        copy.wait_recv()
    send_o(15)
    for c in (chunk(0, 7), chunk(1, 7)):
        complete(c)
        attend(c, 1)
        attend(c, 0)
    complete(15)
    attend(15, 1)

    def close(owner):
        wide = lax.broadcasted_iota(jnp.int32, (QROWS, 2 * KD), 1)
        total = jnp.sum(tot[owner], axis=1, keepdims=True)
        return jnp.where(wide < VD, acc[owner], total)

    acc[1] = close(1)
    home = copies.start(acc.at[1], part, twin)
    attend(15, 0)
    acc[0] = close(0)
    home.wait_recv()
    for h in range(HEADS):
        both = acc[0, h * TOK : (h + 1) * TOK, :] + part[h * TOK : (h + 1) * TOK, :]
        out_ref[:, h * VD : (h + 1) * VD] = (both[:, :VD] / both[:, VD : VD + 1]).astype(BF16)
    for copy in copies.made:
        copy.wait_send()
    assert len(copies.made) <= N_COPIES


def tables():
    frequency = np.exp(np.arange(KD // 2) * (-2.0 * math.log(ROPE_BASE) / KD))

    def both(places):
        angles = places[:, None] * frequency[None, :]
        return np.concatenate([np.cos(angles)] * 2 + [np.sin(angles)] * 2, axis=1).astype(np.float32)

    return both(np.arange(TOK)), both(np.arange(2 * NX * NZ) * TOK)


def on_device(
    dna_bases, stem_weight, stem_bias, conv_weight, conv_bias, norm_gain, query_weight, key_weight, value_weight
):
    marks = (dna_bases + 1).reshape(TOK, 4).T
    marks = jnp.pad(marks, ((0, 4), (0, 64)))
    rope, step = tables()
    vmem = pl.BlockSpec(memory_space=pltpu.VMEM)
    anywhere = pl.BlockSpec(memory_space=pl.ANY)
    return pl.pallas_call(
        kernel,
        out_shape=jax.ShapeDtypeStruct((TOK, HEADS * VD), BF16),
        in_specs=[vmem] * 7 + [anywhere] * 4,
        out_specs=vmem,
        scratch_shapes=[
            pltpu.VMEM((2, 8, 128), jnp.int32),
            pltpu.VMEM((40, 512), F32),
            pltpu.VMEM((40, C1), F32),
            pltpu.VMEM((72, C1), F32),
            pltpu.VMEM((72, C1), F32),
            pltpu.VMEM((2 * TOK, TAPS * C1), BF16),
            pltpu.VMEM((TAPS, C1, C2), BF16),
            pltpu.VMEM((C2, HEADS * KD), BF16),
            pltpu.VMEM((C2, KD), BF16),
            pltpu.VMEM((2 * KD, C2), BF16),
            pltpu.VMEM((16, 8, UROWS, 128), BF16),
            pltpu.VMEM((2, QROWS, KD), BF16),
            pltpu.VMEM((2, QROWS, 2 * KD), F32),
            pltpu.VMEM((2, QROWS, 128), F32),
            pltpu.VMEM((QROWS, 2 * KD), F32),
            pltpu.SemaphoreType.DMA((N_COPIES,)),
            pltpu.SemaphoreType.DMA((N_COPIES,)),
            pltpu.SemaphoreType.DMA((5,)),
        ],
        compiler_params=pltpu.CompilerParams(
            collective_id=0, has_side_effects=True, vmem_limit_bytes=48 << 20
        ),
    )(
        marks, stem_weight, stem_bias.reshape(1, C1), conv_bias.reshape(1, C2), norm_gain.reshape(1, C2),
        jnp.asarray(rope), jnp.asarray(step),
        conv_weight, query_weight, key_weight, value_weight.T,
    )


def solution(mesh):
    placed = (P(("batch", "seq")), P(), P(), P(), P(), P(), P(), P(), P())
    return jax.shard_map(
        on_device, mesh=mesh, in_specs=placed, out_specs=P(("batch", "seq"), None), check_vma=False
    )
```

time: 339 us -> 79.5 us (0.23)
  waiting for transfers between devices: 277 us -> 0 us
  Pallas kernels: 0 us -> 67.8 us
  matrix products: 28.7 us -> 0 us
  starting transfers between devices: 14.4 us -> 0 us
  between operations: 13.7 us -> 0.03 us
  local copies, waits for them, and re-layouts: 1.37 us -> 10.5 us
    all_gather x2 -> x0, waiting for transfers between devices: 275 us -> none  [the longest x1 143 us: on_device(): lax.all_gather(key_rows, 'seq', axis=0, tiled=True)]
    pallas_call x0 -> x1, Pallas kernels: none -> 67.8 us  [on_device(): pl.pallas_call(kernel, out_shape=jax.ShapeDtypeStruct((TOK, HEADS * VD),...]
    dot_general x15 -> x0, matrix products: 28.7 us -> none  [the longest x10 11.2 us: shifted_sum(): jnp.dot(inputs[offset:offset + out_rows], weight[offset], preferred_eleme...]
    ppermute x4 -> x0, starting transfers between devices: 14.4 us -> none  [the longest x2 7.54 us: padded_2(): after = lax.ppermute(initial, axis, down)]
    unnamed x11 -> x15, local copies, waits for them, and re-layouts: 0.08 us -> 8.27 us
  transfers between devices with their start and end apart: 6 -> 0, of which waited for: 4 -> 0; matrix products, arithmetic and copies ran while one was open for 4% -> 0% of each run, Pallas kernels for 0% -> 0%
where the time goes in v1:
time: 79.5 us; the launch traced here: 79 us
  Pallas kernels  67.8 us (85%)
  local copies, waits for them, and re-layouts  10.5 us (13%)
    pallas_call x1, Pallas kernels, on_device(): pl.pallas_call(kernel, out_shape=jax.ShapeDtypeStruct((TOK, HEADS * VD),...  67.8 us
    unnamed x15, local copies, waits for them, and re-layouts  8.27 us

profile of v1, /device:TPU:1, one launch (start us, length us, event | category | flops | bytes accessed | tf_op | source)
XLA Modules:
  0.0 79.0 jit_solution(18156012749390992578)
XLA Ops:
  0.0 0.7 broadcast_add_fusion
  0.7 0.7 reshape.13.stem_b_ref
  1.4 0.7 reshape.14.conv_b_ref
  2.1 0.7 reshape.15.gain_ref
  2.7 0.1 reshape.12
  2.9 0.1 copy.12
  2.9 0.0 copy-start
  2.9 1.8 %copy-done = bf16[5,384,768]{2,1,0:T(8,128)(2,1)S(1)} copy-done((bf16[5,384,768]{2,1,0:T(8,128)(2,1)S(1)}, bf16[5,384,768]{2,1,0:T(8,128)(2,1)}, u32[]{:S(2)}) %copy-start) | copy-done | bytes 2949144
  4.8 0.0 copy-start.1
  4.8 1.4 %copy-done.1 = bf16[768,1024]{1,0:T(8,128)(2,1)S(1)} copy-done((bf16[768,1024]{1,0:T(8,128)(2,1)S(1)}, bf16[768,1024]{1,0:T(8,128)(2,1)}, u32[]{:S(2)}) %copy-start.1) | copy-done | bytes 1572888
  6.2 0.0 copy-start.2
  6.2 1.0 %copy-done.2 = bf16[768,192]{0,1:T(8,128)(2,1)S(1)} copy-done((bf16[768,192]{0,1:T(8,128)(2,1)S(1)}, bf16[768,192]{0,1:T(8,128)(2,1)}, u32[]{:S(2)}) %copy-start.2) | copy-done | bytes 294936
  7.1 0.0 copy-start.3
  7.2 0.9 %copy-done.3 = bf16[768,128]{1,0:T(8,128)(2,1)S(1)} copy-done((bf16[768,128]{1,0:T(8,128)(2,1)S(1)}, bf16[768,128]{1,0:T(8,128)(2,1)}, u32[]{:S(2)}) %copy-start.3) | copy-done | bytes 196632
  8.1 0.0 copy-start.4
  8.1 0.9 %copy-done.4 = f32[128,256]{1,0:T(8,128)S(1)} copy-done((f32[128,256]{1,0:T(8,128)S(1)}, f32[128,256]{1,0:T(8,128)}, u32[]{:S(2)}) %copy-start.4) | copy-done | bytes 131096
  9.0 0.0 copy-start.5
  9.0 0.8 %copy-done.5 = f32[64,256]{1,0:T(8,128)S(1)} copy-done((f32[64,256]{1,0:T(8,128)S(1)}, f32[64,256]{1,0:T(8,128)}, u32[]{:S(2)}) %copy-start.5) | copy-done | bytes 65560
  9.8 0.0 copy-start.6
  9.8 0.7 copy-done.6
  10.5 67.8 %shard_map.109 = bf16[64,1536]{1,0:T(8,128)(2,1)S(1)} custom-call(s32[8,128]{1,0:T(8,128)S(1)} %pad.4.bases_ref, bf16[5,4,384]{2,1,0:T(4,128)(2,1)S(1)} %copy-done.6, f32[1,384]{1,0:T(1,128)S(1)} %reshape.13.stem_b_ref, f32[1,768]{1,0:T(1,128)S(1)} %reshape.14.conv_b_ref, f32[1,768]{1,0:T(1,128)S(1)} %reshape.15.gain_ref, f32[64,256]{1,0:T(8,128)S(1)} %copy-done.5, ...), custom_call_target="tpu_custom_call" | custom-call | tf_op jit(solution)/shard_map/pallas_call | solution.py:326
  78.4 0.7 copy.14
  (1 shorter events, 0.0 us)
Async XLA Ops:
  2.9 1.8 %copy-start = (bf16[5,384,768]{2,1,0:T(8,128)(2,1)S(1)}, bf16[5,384,768]{2,1,0:T(8,128)(2,1)}, u32[]{:S(2)}) copy-start(bf16[5,384,768]{2,1,0:T(8,128)(2,1)} %conv_w_hbm.1) | copy-start | bytes 8847364
  4.8 1.4 %copy-start.1 = (bf16[768,1024]{1,0:T(8,128)(2,1)S(1)}, bf16[768,1024]{1,0:T(8,128)(2,1)}, u32[]{:S(2)}) copy-start(bf16[768,1024]{1,0:T(8,128)(2,1)} %query_w_hbm.1) | copy-start | bytes 4718596
  6.2 1.0 %copy-start.2 = (bf16[768,192]{0,1:T(8,128)(2,1)S(1)}, bf16[768,192]{0,1:T(8,128)(2,1)}, u32[]{:S(2)}) copy-start(bf16[768,192]{0,1:T(8,128)(2,1)} %param.19) | copy-start | bytes 884740
  7.1 0.9 %copy-start.3 = (bf16[768,128]{1,0:T(8,128)(2,1)S(1)}, bf16[768,128]{1,0:T(8,128)(2,1)}, u32[]{:S(2)}) copy-start(bf16[768,128]{1,0:T(8,128)(2,1)} %key_w_hbm.1) | copy-start | bytes 589828
  8.1 0.9 %copy-start.4 = (f32[128,256]{1,0:T(8,128)S(1)}, f32[128,256]{1,0:T(8,128)}, u32[]{:S(2)}) copy-start(f32[128,256]{1,0:T(8,128)} %constant.9.clone.step_ref) | copy-start | bytes 393220
  9.0 0.8 %copy-start.5 = (f32[64,256]{1,0:T(8,128)S(1)}, f32[64,256]{1,0:T(8,128)}, u32[]{:S(2)}) copy-start(f32[64,256]{1,0:T(8,128)} %constant.8.clone.rope_ref) | copy-start | bytes 196612
  9.8 0.7 copy-start.6

commit v2 on v1

v2 whole, which is shorter than its diff:
```python
import functools
import math

import jax
import jax.numpy as jnp
import numpy as np
from jax import lax
from jax.experimental import pallas as pl
from jax.experimental.pallas import tpu as pltpu
from jax.sharding import PartitionSpec as P

MESH = pl.DeviceIdType.MESH
SOFT_CAP = 20.0
ROPE_BASE = 10000.0
NX, NZ = 4, 16
TOK = 64
C1, C2, HEADS, KD, VD, TAPS = 384, 768, 8, 128, 192, 5
UROWS = 80
QROWS = TOK * HEADS
F32, BF16 = jnp.float32, jnp.bfloat16

U_C, U_L2, U_L1, U_R1, U_R2, U_O = 0, 2, 3, 4, 5, 6

ORDER = (0, 1, -1, 2, -2, 5, -5, 4, -4, 6, -6, 3, -3, 7, -7, 8)
NEAR = (1, -1, 2, -2)


def gelu(x):
    inner = math.sqrt(2.0 / math.pi) * (x + 0.044715 * (x * x * x))
    return (0.5 * x) * (1.0 + jnp.tanh(inner))


class Copies:
    def __init__(self, send, recv):
        self.send, self.recv, self.made = send, recv, []

    def start(self, src, dst, to):
        k = len(self.made)
        copy = pltpu.make_async_remote_copy(
            src_ref=src, dst_ref=dst, send_sem=self.send.at[k], recv_sem=self.recv.at[k],
            device_id={"seq": to}, device_id_type=MESH,
        )
        copy.start()
        self.made.append(copy)
        return copy


N_COPIES = 96


def kernel(
    bases_hbm, stem_w_hbm, stem_b_hbm, conv_b_hbm, gain_hbm, rope_hbm, step_hbm,
    conv_w_hbm, query_w_hbm, key_w_hbm, value_w_hbm,
    out_ref,
    bases_ref, stem_w_ref, stem_b_ref, conv_b_ref, gain_ref, rope_ref, step_ref,
    halo, onehot, stem_w, pooled_e, pooled_o, conv_in, conv_w, query_w, key_w, value_w,
    buf, q_buf, acc, tot, part, send, recv, load,
):
    me = lax.axis_index("seq")
    core, z, x = me % 2, (me // 2) % NZ, me // (2 * NZ)

    def at(xx, zz, cc):
        return ((xx % NX) * NZ + zz % NZ) * 2 + cc

    x_up, x_down = at(x + 1, z, core), at(x + NX - 1, z, core)
    z_up, z_down = at(x, z + 1, core), at(x, z + NZ - 1, core)
    z_far_up, z_far_down = at(x, z + 5, core), at(x, z + NZ - 5, core)
    twin = at(x, z, 1 - core)
    after, before = (me + 1) % (2 * NX * NZ), (me + 2 * NX * NZ - 1) % (2 * NX * NZ)
    other = jnp.where(core == 0, before, after)

    first_loads = [
        pltpu.make_async_copy(bases_hbm.at[pl.ds(0, 128)], bases_ref.at[0], load.at[5]),
        pltpu.make_async_copy(bases_hbm.at[pl.ds(128, 128)], bases_ref.at[1], load.at[6]),
        pltpu.make_async_copy(stem_w_hbm, stem_w_ref, load.at[7]),
        pltpu.make_async_copy(stem_b_hbm, stem_b_ref, load.at[8]),
        pltpu.make_async_copy(rope_hbm, rope_ref, load.at[9]),
        pltpu.make_async_copy(step_hbm.at[pl.ds(me, 1)], step_ref, load.at[10]),
        pltpu.make_async_copy(conv_b_hbm, conv_b_ref, load.at[11]),
        pltpu.make_async_copy(gain_hbm, gain_ref, load.at[12]),
    ]
    for one in first_loads:
        one.start()
    loads = [
        pltpu.make_async_copy(conv_w_hbm, conv_w, load.at[0]),
        pltpu.make_async_copy(key_w_hbm, key_w, load.at[1]),
        pltpu.make_async_copy(value_w_hbm, value_w.at[pl.ds(0, VD)], load.at[2]),
        pltpu.make_async_copy(value_w_hbm.at[pl.ds(KD, VD - KD)], value_w.at[pl.ds(VD, VD - KD)], load.at[3]),
        pltpu.make_async_copy(query_w_hbm, query_w, load.at[4]),
    ]
    for one in loads:
        one.start()

    barrier = pltpu.get_barrier_semaphore()
    for peer in (x_up, x_down, z_up, z_down, z_far_up, z_far_down, twin, other):
        pl.semaphore_signal(barrier, inc=1, device_id={"seq": peer}, device_id_type=MESH)
    for one in first_loads:
        one.wait()
    pl.semaphore_wait(barrier, 8)

    copies = Copies(send, recv)
    from_before = copies.start(bases_ref, halo.at[0], after)
    from_after = copies.start(bases_ref, halo.at[1], before)

    stem_w[...] = jnp.zeros_like(stem_w)
    for t in range(TAPS):
        stem_w[t * 8 : t * 8 + 4, :] = stem_w_ref[t].astype(F32)
    dev = step_ref[...]
    cos_d, sin_d = dev[:, :KD], dev[:, KD:]
    cos_r, sin_r = rope_ref[:, :KD], rope_ref[:, KD:]
    lane = lax.broadcasted_iota(jnp.int32, (TOK, KD), 1)
    cos = cos_d * cos_r - sin_d * sin_r
    sin = sin_d * cos_r + cos_d * sin_r
    sin = jnp.where(lane < KD // 2, -sin, sin)

    def rotate(u):
        return u * cos + pltpu.roll(u, KD // 2, 1) * sin

    from_before.wait_recv()
    from_after.wait_recv()

    near = [
        jnp.where(me == 0, 0, halo[0, 1:2, :] + 1),
        bases_ref[0:1, :] + 1,
        bases_ref[1:2, :] + 1,
        jnp.where(me == 2 * NX * NZ - 1, 0, halo[1, 0:1, :] + 1),
    ]
    phase = (lax.broadcasted_iota(jnp.int32, (8, 128), 1) & 3) == lax.broadcasted_iota(jnp.int32, (8, 128), 0)
    spot = lax.broadcasted_iota(jnp.int32, (128, 128), 0)
    token = lax.broadcasted_iota(jnp.int32, (128, 128), 1)
    marks = jnp.zeros((8, 128), F32)
    for b in range(4):
        picked = jnp.where(phase, jnp.broadcast_to(near[b], (8, 128)), 0).astype(F32).astype(BF16)
        place = (((spot + (128 * b - 120)) >> 2) == token).astype(F32).astype(BF16)
        marks += jnp.dot(picked, place, preferred_element_type=F32)
    moved = [marks, pltpu.roll(marks, 127, 1), pltpu.roll(marks, 126, 1)]
    base = (lax.broadcasted_iota(jnp.int32, (8, 128), 0) + 1).astype(F32)
    for r in range(4):
        for t in range(TAPS):
            k = r + t - 2
            row = moved[1 + k // 4][k % 4 : k % 4 + 1, :]
            onehot[t * 8 : t * 8 + 8, r * 128 : (r + 1) * 128] = (
                jnp.broadcast_to(row, (8, 128)) == base
            ).astype(F32)
    stem = lax.dot_general(
        onehot[...].astype(BF16), stem_w[...].astype(BF16), (((0,), (0,)), ((), ())),
        preferred_element_type=F32,
    )
    stem = [gelu(stem[r * 128 : r * 128 + 72] + stem_b_ref[...].reshape(1, C1)) for r in range(4)]
    spot = lax.broadcasted_iota(jnp.int32, (72, C1), 0)
    first = jnp.where(me == 0, 1, 0)
    last = jnp.where(me == 2 * NX * NZ - 1, 64, 65)
    inside = (spot >= first) & (spot <= last)
    pooled_e[...] = jnp.where(inside, jnp.maximum(stem[0], stem[1]), 0.0)
    pooled_o[...] = jnp.where(inside, jnp.maximum(stem[2], stem[3]), 0.0)

    shifted = [[ref[pl.ds(o, TOK), :].astype(BF16) for ref in (pooled_e, pooled_o)] for o in range(3)]
    for t in range(TAPS):
        conv_in[0:TOK, t * C1 : (t + 1) * C1] = shifted[t // 2][t % 2]
        conv_in[TOK : 2 * TOK, t * C1 : (t + 1) * C1] = shifted[(t + 1) // 2][(t + 1) % 2]
    loads[0].wait()
    conv = jnp.dot(
        conv_in[...], conv_w[...].reshape(TAPS * C1, C2), preferred_element_type=F32
    ) + conv_b_ref[...].reshape(1, C2)
    conv = gelu(conv)
    features = jnp.maximum(conv[:TOK], conv[TOK:])
    mean_square = jnp.mean(features * features, axis=1, keepdims=True)
    normed = (features * lax.rsqrt(mean_square + 1e-06) * gain_ref[...].reshape(1, C2)).astype(BF16)

    for one in loads[1:4]:
        one.wait()
    keys = rotate(jnp.dot(normed, key_w[...], preferred_element_type=F32)).astype(BF16)
    values = lax.dot_general(normed, value_w[...], (((1,), (1,)), ((), ())), preferred_element_type=F32)
    tails = values[:, KD:]
    values = values[:, :KD].astype(BF16)
    half = lax.broadcasted_iota(jnp.int32, (16, KD), 1) < KD // 2
    for u in range(2):
        buf[0, u, 0:32, :] = keys[u * 32 : u * 32 + 32]
        buf[0, u, 32:64, :] = values[u * 32 : u * 32 + 32]
        buf[0, u, 64:80, :] = jnp.where(
            half, tails[u * 32 : u * 32 + 16], tails[u * 32 + 16 : u * 32 + 32]
        ).astype(BF16)

    def units(d, u, n=1):
        return buf.at[ORDER.index(d), pl.ds(u, n)]

    arrive_a, arrive_b, arrive_x, arrive_o = {}, {}, {}, {}

    def send_a(src, dst, to):
        arrive_a[dst] = copies.start(units(src, U_C, 2), units(dst, U_C, 2), to)

    def send_b(src, dst, to):
        u, n = (U_L1, 2) if dst in NEAR else (U_L1, 1) if 0 < dst < 8 else (U_R1, 1)
        arrive_b[dst] = copies.start(units(src, u, n), units(dst, u, n), to)

    def send_x(d):
        left, right = (U_C + 1, U_L2, 1), (U_C + 1, U_R2, 1)
        if 0 < d < 8 and d not in NEAR:
            right = (U_C, U_R1, 2)
        elif d not in NEAR:
            left = (U_C, U_L2, 2)
        arrive_x[d] = [
            copies.start(units(d, u, n), units(d, v, n), to)
            for (u, v, n), to in ((left, x_up), (right, x_down))
        ]

    def send_o(d):
        if d == 0:
            sends = ((U_L1, U_O, 1, x_up), (U_R2, U_O + 1, 1, x_down))
        elif 0 < d < 8:
            sends = ((U_L2, U_O, 2, x_up),)
        else:
            sends = ((U_R1, U_O, 2, x_down),)
        arrive_o[d] = [copies.start(units(d, u, n), units(d, v, n), to) for u, v, n, to in sends]

    def onward(d, send):
        if d in (1, 5, 6):
            send(d, d + 1, z_up)
        if d in (-1, -5, -6):
            send(d, d - 1, z_down)
        if d in (5, 4):
            send(d, d - 1, z_down)
        if d in (-5, -4):
            send(d, d + 1, z_up)
        if d == 7 and send is send_a:
            send(d, 8, z_up)
        if d == -7 and send is send_b:
            send(d, 8, z_down)

    send_a(0, 5, z_far_up)
    send_a(0, -5, z_far_down)
    arrive_x[0] = [
        copies.start(units(0, u, n), units(0, v, n), to)
        for u, v, n, to in ((U_C, U_L1, 1, x_up), (U_C, U_R1, 2, x_down), (U_C + 1, U_L2, 1, x_up))
    ]
    send_a(0, 1, z_up)
    send_a(0, -1, z_down)

    def take_a(*chunks):
        for d in chunks:
            arrive_a[d].wait_recv()
            onward(d, send_a)
            send_x(d)

    def take_b(*chunks):
        for d in chunks:
            arrive_b[d].wait_recv()
            onward(d, send_b)

    def take_x(*chunks):
        for d in chunks:
            for copy in arrive_x[d]:
                copy.wait_recv()
            send_o(d)

    loads[4].wait()
    for h in range(HEADS):
        u = jnp.dot(normed, query_w[:, h * KD : (h + 1) * KD], preferred_element_type=F32)
        q_buf[h * TOK : (h + 1) * TOK, :] = rotate(u).astype(BF16)
    queries = copies.start(q_buf.at[pl.ds(0, QROWS)], q_buf.at[pl.ds(QROWS, QROWS)], twin)

    take_x(0)
    send_b(0, 5, z_far_up)
    send_b(0, -5, z_far_down)
    send_b(0, 1, z_up)
    send_b(0, -1, z_down)
    take_a(1, -1)
    acc[...] = jnp.zeros_like(acc)
    tot[...] = jnp.zeros_like(tot)
    queries.wait_recv()

    scale = 1.0 / math.sqrt(KD) / SOFT_CAP
    peak = SOFT_CAP * math.log2(math.e)
    rows, width = 256, 512

    def attend(tile, blocks):
        for d in ORDER[2 * tile : 2 * tile + 2]:
            for copy in arrive_o.pop(d, ()):
                copy.wait_recv()
        key_rows = buf[2 * tile : 2 * tile + 2, :, 0:32, :].reshape(width, KD)
        value_rows = buf[2 * tile : 2 * tile + 2, :, 32:64, :].reshape(width, KD)
        tail = buf[2 * tile : 2 * tile + 2, :, 64:80, :].reshape(width // 32, 16, KD)
        turned = pltpu.roll(tail.astype(F32).reshape(width // 2, KD), KD // 2, 1)
        turned = turned.astype(BF16).reshape(width // 32, 16, KD)
        tail = jnp.concatenate([tail, turned], axis=1).reshape(width, KD)
        right_side = jnp.concatenate([value_rows, tail], axis=1)
        for i in blocks:
            at_rows = pl.ds(i * rows, rows)
            scores = lax.dot_general(
                q_buf[at_rows, :], key_rows, (((1,), (1,)), ((), ())), preferred_element_type=F32
            )
            probability = jnp.exp2(jnp.tanh(scores * scale) * peak - peak)
            tot[at_rows, :] += sum(probability[:, j : j + 128] for j in range(0, width, 128))
            acc[at_rows, :] += jnp.dot(probability.astype(BF16), right_side, preferred_element_type=F32)

    every = range(2 * QROWS // rows)
    take_a(5, -5, 2, -2)
    take_b(1, -1)
    take_x(1, -1)
    take_a(6, -6, 4, -4)
    take_b(5, -5, 2, -2)
    take_x(5, -5, 2, -2)
    attend(0, every)
    take_a(7, -7, 3, -3)
    take_b(6, -6, 4, -4)
    take_x(6, -6, 4, -4)
    attend(1, every)
    attend(2, every)
    take_a(8)
    take_b(7, -7, 3, -3)
    take_x(7, -7, 3, -3)
    attend(3, every)
    attend(4, every)
    take_b(8)
    take_x(8)
    attend(5, every)
    attend(6, every)

    wide = lax.broadcasted_iota(jnp.int32, (rows, 2 * KD), 1)
    home = []
    for i in (2, 3):
        attend(7, (i,))
        at_rows = pl.ds(i * rows, rows)
        total = jnp.sum(tot[at_rows, :], axis=1, keepdims=True)
        acc[at_rows, :] = jnp.where(wide < VD, acc[at_rows, :], total)
        home.append(copies.start(acc.at[at_rows], part.at[pl.ds((i - 2) * rows, rows)], twin))
    attend(7, (0, 1))
    for h in range(HEADS):
        if h % 4 == 0:
            home[h // 4].wait_recv()
        at_rows = pl.ds(h * TOK, TOK)
        both = acc[at_rows, :VD] + part[at_rows, :VD]
        total = jnp.sum(tot[at_rows, :], axis=1, keepdims=True) + part[at_rows, VD : VD + 1]
        out_ref[:, h * VD : (h + 1) * VD] = (both * (1.0 / total)).astype(BF16)
    for copy in copies.made:
        copy.wait_send()
    assert len(copies.made) <= N_COPIES


def tables():
    frequency = np.exp(np.arange(KD // 2) * (-2.0 * math.log(ROPE_BASE) / KD))

    def both(places):
        angles = places[:, None] * frequency[None, :]
        return np.concatenate([np.cos(angles)] * 2 + [np.sin(angles)] * 2, axis=1).astype(np.float32)

    return both(np.arange(TOK)), both(np.arange(2 * NX * NZ) * TOK)


def on_device(
    dna_bases, stem_weight, stem_bias, conv_weight, conv_bias, norm_gain, query_weight, key_weight, value_weight
):
    rope, step = tables()
    vmem = pl.BlockSpec(memory_space=pltpu.VMEM)
    anywhere = pl.BlockSpec(memory_space=pl.ANY)
    return pl.pallas_call(
        kernel,
        out_shape=jax.ShapeDtypeStruct((TOK, HEADS * VD), BF16),
        in_specs=[anywhere] * 11,
        out_specs=vmem,
        scratch_shapes=[
            pltpu.VMEM((2, 128), jnp.int32),
            pltpu.VMEM((TAPS, 4, C1), BF16),
            pltpu.VMEM((C1,), F32),
            pltpu.VMEM((C2,), F32),
            pltpu.VMEM((C2,), F32),
            pltpu.VMEM((TOK, 2 * KD), F32),
            pltpu.VMEM((1, 2 * KD), F32),
            pltpu.VMEM((2, 2, 128), jnp.int32),
            pltpu.VMEM((40, 512), F32),
            pltpu.VMEM((40, C1), F32),
            pltpu.VMEM((72, C1), F32),
            pltpu.VMEM((72, C1), F32),
            pltpu.VMEM((2 * TOK, TAPS * C1), BF16),
            pltpu.VMEM((TAPS, C1, C2), BF16),
            pltpu.VMEM((C2, HEADS * KD), BF16),
            pltpu.VMEM((C2, KD), BF16),
            pltpu.VMEM((2 * KD, C2), BF16),
            pltpu.VMEM((16, 8, UROWS, 128), BF16),
            pltpu.VMEM((2 * QROWS, KD), BF16),
            pltpu.VMEM((2 * QROWS, 2 * KD), F32),
            pltpu.VMEM((2 * QROWS, 128), F32),
            pltpu.VMEM((QROWS, 2 * KD), F32),
            pltpu.SemaphoreType.DMA((N_COPIES,)),
            pltpu.SemaphoreType.DMA((N_COPIES,)),
            pltpu.SemaphoreType.DMA((13,)),
        ],
        compiler_params=pltpu.CompilerParams(
            collective_id=0, has_side_effects=True, vmem_limit_bytes=62 << 20
        ),
    )(
        dna_bases, stem_weight, stem_bias, conv_bias, norm_gain,
        jnp.asarray(rope), jnp.asarray(step),
        conv_weight, query_weight, key_weight, value_weight.T,
    )


def solution(mesh):
    placed = (P(("batch", "seq")), P(), P(), P(), P(), P(), P(), P(), P())
    return jax.shard_map(
        on_device, mesh=mesh, in_specs=placed, out_specs=P(("batch", "seq"), None), check_vma=False
    )
```

time: 79.5 us -> 54.7 us (0.69)
  Pallas kernels: 67.8 us -> 52.9 us
  local copies, waits for them, and re-layouts: 10.5 us -> 1.62 us
    pallas_call x1, Pallas kernels: 67.8 us -> 52.9 us  [on_device(): pl.pallas_call(kernel, out_shape=jax.ShapeDtypeStruct((TOK, HEADS * VD),...]
    unnamed x15 -> x1, local copies, waits for them, and re-layouts: 8.27 us -> 1.62 us
    reshape x5 -> x0, local copies, waits for them, and re-layouts: 2.23 us -> none  [the longest x1 0.69 us: on_device(): norm_gain.reshape(1, C2)]
where the time goes in v2:
time: 54.7 us; the launch traced here: 54.6 us
  Pallas kernels  52.9 us (97%)
  local copies, waits for them, and re-layouts  1.62 us (3%)
    pallas_call x1, Pallas kernels, on_device(): pl.pallas_call(kernel, out_shape=jax.ShapeDtypeStruct((TOK, HEADS * VD),...  52.9 us
    unnamed x1, local copies, waits for them, and re-layouts  1.62 us

profile of v2, /device:TPU:1, one launch (start us, length us, event | category | flops | bytes accessed | tf_op | source)
XLA Modules:
  0.0 54.6 jit_solution(5306802352326370155)
XLA Ops:
  0.0 52.9 %shard_map.109 = bf16[64,1536]{1,0:T(8,128)(2,1)} custom-call(s32[256]{0:T(256)} %bases_hbm.1, bf16[5,4,384]{2,1,0:T(4,128)(2,1)} %stem_w_hbm.1, f32[384]{0:T(512)} %stem_b_hbm.1, f32[768]{0:T(1024)} %conv_b_hbm.1, f32[768]{0:T(1024)} %gain_hbm.1, f32[64,256]{1,0:T(8,128)} %constant.4.clone.rope_hbm, f32[128,256]{1,0:T(8,128)} %constant.5.clone.step_hbm, ...), custom_call_target="tpu_custom_call" | custom-call | tf_op jit(solution)/shard_map/pallas_call | solution.py:356
  52.9 1.6 %copy.13 = bf16[64,1536]{1,0:T(8,128)(2,1)} copy(bf16[64,1536]{1,0:T(8,128)(2,1)} %shard_map.109) | data formatting | bytes 393216

commit v3 on v2

--- a/solution.py
+++ b/solution.py
@@ -21,8 +21,11 @@
 
 U_C, U_L2, U_L1, U_R1, U_R2, U_O = 0, 2, 3, 4, 5, 6
 
-ORDER = (0, 1, -1, 2, -2, 5, -5, 4, -4, 6, -6, 3, -3, 7, -7, 8)
+ORDER = (0, 1, -1, 5, -5, 2, -2, 6, -6, 4, -4, 7, -7, 3, -3, 8)
 NEAR = (1, -1, 2, -2)
+SEED = 5
+STAGES = ((1, -1), (5, -5, 2, -2), (6, -6, 4, -4), (7, -7, 3, -3), (8,))
+UP, BACK = {1: 2, 5: 6, 6: 7}, {5: 4, 4: 3}
 
 
 def gelu(x):
@@ -64,7 +67,7 @@
 
     x_up, x_down = at(x + 1, z, core), at(x + NX - 1, z, core)
     z_up, z_down = at(x, z + 1, core), at(x, z + NZ - 1, core)
-    z_far_up, z_far_down = at(x, z + 5, core), at(x, z + NZ - 5, core)
+    z_far_up, z_far_down = at(x, z + SEED, core), at(x, z + NZ - SEED, core)
     twin = at(x, z, 1 - core)
     after, before = (me + 1) % (2 * NX * NZ), (me + 2 * NX * NZ - 1) % (2 * NX * NZ)
     other = jnp.where(core == 0, before, after)
@@ -214,21 +217,17 @@
         arrive_o[d] = [copies.start(units(d, u, n), units(d, v, n), to) for u, v, n, to in sends]
 
     def onward(d, send):
-        if d in (1, 5, 6):
-            send(d, d + 1, z_up)
-        if d in (-1, -5, -6):
-            send(d, d - 1, z_down)
-        if d in (5, 4):
-            send(d, d - 1, z_down)
-        if d in (-5, -4):
-            send(d, d + 1, z_up)
-        if d == 7 and send is send_a:
-            send(d, 8, z_up)
-        if d == -7 and send is send_b:
-            send(d, 8, z_down)
-
-    send_a(0, 5, z_far_up)
-    send_a(0, -5, z_far_down)
+        away, back = (z_up, z_down) if d > 0 else (z_down, z_up)
+        sign = 1 if d > 0 else -1
+        if abs(d) in UP:
+            send(d, sign * UP[abs(d)], away)
+        if abs(d) in BACK:
+            send(d, sign * BACK[abs(d)], back)
+        if d == (7 if send is send_a else -7):
+            send(d, 8, away)
+
+    send_a(0, SEED, z_far_up)
+    send_a(0, -SEED, z_far_down)
     arrive_x[0] = [
         copies.start(units(0, u, n), units(0, v, n), to)
         for u, v, n, to in ((U_C, U_L1, 1, x_up), (U_C, U_R1, 2, x_down), (U_C + 1, U_L2, 1, x_up))
@@ -260,11 +259,11 @@
     queries = copies.start(q_buf.at[pl.ds(0, QROWS)], q_buf.at[pl.ds(QROWS, QROWS)], twin)
 
     take_x(0)
-    send_b(0, 5, z_far_up)
-    send_b(0, -5, z_far_down)
+    send_b(0, SEED, z_far_up)
+    send_b(0, -SEED, z_far_down)
     send_b(0, 1, z_up)
     send_b(0, -1, z_down)
-    take_a(1, -1)
+    take_a(*STAGES[0])
     acc[...] = jnp.zeros_like(acc)
     tot[...] = jnp.zeros_like(tot)
     queries.wait_recv()
@@ -294,27 +293,19 @@
             acc[at_rows, :] += jnp.dot(probability.astype(BF16), right_side, preferred_element_type=F32)
 
     every = range(2 * QROWS // rows)
-    take_a(5, -5, 2, -2)
-    take_b(1, -1)
-    take_x(1, -1)
-    take_a(6, -6, 4, -4)
-    take_b(5, -5, 2, -2)
-    take_x(5, -5, 2, -2)
-    attend(0, every)
-    take_a(7, -7, 3, -3)
-    take_b(6, -6, 4, -4)
-    take_x(6, -6, 4, -4)
-    attend(1, every)
-    attend(2, every)
-    take_a(8)
-    take_b(7, -7, 3, -3)
-    take_x(7, -7, 3, -3)
-    attend(3, every)
-    attend(4, every)
-    take_b(8)
-    take_x(8)
-    attend(5, every)
-    attend(6, every)
+    tile = 0
+    for k in range(1, len(STAGES) + 1):
+        if k < len(STAGES):
+            take_a(*STAGES[k])
+        take_b(*STAGES[k - 1])
+        take_x(*STAGES[k - 1])
+        known = 1 + sum(len(stage) for stage in STAGES[: k - 1])
+        while tile < min(known // 2, 7):
+            attend(tile, every)
+            tile += 1
+    while tile < 7:
+        attend(tile, every)
+        tile += 1
 
     wide = lax.broadcasted_iota(jnp.int32, (rows, 2 * KD), 1)
     home = []
@@ -352,7 +343,7 @@
 ):
     rope, step = tables()
     vmem = pl.BlockSpec(memory_space=pltpu.VMEM)
-    anywhere = pl.BlockSpec(memory_space=pl.ANY)
+    anywhere = pl.BlockSpec(memory_space=pltpu.HBM)
     return pl.pallas_call(
         kernel,
         out_shape=jax.ShapeDtypeStruct((TOK, HEADS * VD), BF16),
@@ -386,13 +377,15 @@
             pltpu.SemaphoreType.DMA((13,)),
         ],
         compiler_params=pltpu.CompilerParams(
-            collective_id=0, has_side_effects=True, vmem_limit_bytes=62 << 20
+            collective_id=0, has_side_effects=True, vmem_limit_bytes=44 << 20
         ),
-    )(
-        dna_bases, stem_weight, stem_bias, conv_bias, norm_gain,
-        jnp.asarray(rope), jnp.asarray(step),
-        conv_weight, query_weight, key_weight, value_weight.T,
-    )
+    )(*(
+        pltpu.with_memory_space_constraint(one, pltpu.HBM)
+        for one in (
+            dna_bases, stem_weight, stem_bias, conv_bias, norm_gain, jnp.asarray(rope), jnp.asarray(step),
+            conv_weight, query_weight, key_weight, value_weight.T,
+        )
+    ))
 
 
 def solution(mesh):

time: 54.7 us -> 52.6 us (0.962)
  Pallas kernels: 52.9 us -> 51.8 us
  local copies, waits for them, and re-layouts: 1.62 us -> 0.68 us
    pallas_call x1, Pallas kernels: 52.9 us -> 51.8 us  [on_device(): pl.pallas_call(kernel, out_shape=jax.ShapeDtypeStruct((TOK, HEADS * VD),...]
    unnamed x1, local copies, waits for them, and re-layouts: 1.62 us -> 0.68 us
where the time goes in v3:
time: 52.6 us; the launch traced here: 52.5 us
  Pallas kernels  51.8 us (98%)
  local copies, waits for them, and re-layouts  0.68 us (1%)
    pallas_call x1, Pallas kernels, on_device(): pl.pallas_call(kernel, out_shape=jax.ShapeDtypeStruct((TOK, HEADS * VD),...  51.8 us

profile of v3, /device:TPU:1, one launch (start us, length us, event | category | flops | bytes accessed | tf_op | source)
XLA Modules:
  0.0 52.5 jit_solution(16411608232097386363)
XLA Ops:
  0.0 51.8 %shard_map.109 = bf16[64,1536]{1,0:T(8,128)(2,1)S(1)} custom-call(s32[256]{0:T(256)} %bases_hbm.1, bf16[5,4,384]{2,1,0:T(4,128)(2,1)} %stem_w_hbm.1, f32[384]{0:T(512)} %stem_b_hbm.1, f32[768]{0:T(1024)} %conv_b_hbm.1, f32[768]{0:T(1024)} %gain_hbm.1, f32[64,256]{1,0:T(8,128)} %constant.4.clone.rope_hbm, f32[128,256]{1,0:T(8,128)} %constant.5.clone.step_hbm, ...), custom_call_target="tpu_custom_call" | custom-call | tf_op jit(solution)/shard_map/pallas_call | solution.py:347
  51.8 0.7 %copy.13 = bf16[64,1536]{1,0:T(8,128)(2,1)} copy(bf16[64,1536]{1,0:T(8,128)(2,1)S(1)} %shard_map.109) | data formatting | bytes 393216

commit v4 on v3

--- a/solution.py
+++ b/solution.py
@@ -19,13 +19,25 @@
 QROWS = TOK * HEADS
 F32, BF16 = jnp.float32, jnp.bfloat16
 
-U_C, U_L2, U_L1, U_R1, U_R2, U_O = 0, 2, 3, 4, 5, 6
+U_C, U_L, U_R, U_O = 0, 2, 4, 6
 
 ORDER = (0, 1, -1, 5, -5, 2, -2, 6, -6, 4, -4, 7, -7, 3, -3, 8)
-NEAR = (1, -1, 2, -2)
+OVER_Z = {1: 2, -1: 2, 2: 2, -2: 2, 5: 2, -5: 2, 6: 4, -6: 4, 4: 4, -4: 4, 7: 4, -7: 4, 3: 4, -3: 4, 8: 2}
 SEED = 5
-STAGES = ((1, -1), (5, -5, 2, -2), (6, -6, 4, -4), (7, -7, 3, -3), (8,))
+STAGES = ((1, -1), (5, -5, 2, -2), (6, -6, 4, -4), (7, -7, 3, -3, 8))
 UP, BACK = {1: 2, 5: 6, 6: 7}, {5: 4, 4: 3}
+
+
+def over_z(d):
+    ahead = 0 < d < 8
+    return {
+        2: (U_L, 0), 3: (U_L + 1, 1) if ahead else (U_R, 1), 4: (U_L + 1, 2), 5: (U_L, 3) if ahead else (U_L + 1, 3)
+    }[OVER_Z.get(d, 2)]
+
+
+def covers(src, dst):
+    (u, n), (v, m) = over_z(src), over_z(dst)
+    return src != 0 and u <= v and v + m <= u + n
 
 
 def gelu(x):
@@ -68,6 +80,7 @@
     x_up, x_down = at(x + 1, z, core), at(x + NX - 1, z, core)
     z_up, z_down = at(x, z + 1, core), at(x, z + NZ - 1, core)
     z_far_up, z_far_down = at(x, z + SEED, core), at(x, z + NZ - SEED, core)
+    z_three_up, z_three_down = at(x, z + 8 - SEED, core), at(x, z + NZ - 8 + SEED, core)
     twin = at(x, z, 1 - core)
     after, before = (me + 1) % (2 * NX * NZ), (me + 2 * NX * NZ - 1) % (2 * NX * NZ)
     other = jnp.where(core == 0, before, after)
@@ -95,11 +108,11 @@
         one.start()
 
     barrier = pltpu.get_barrier_semaphore()
-    for peer in (x_up, x_down, z_up, z_down, z_far_up, z_far_down, twin, other):
+    for peer in (x_up, x_down, z_up, z_down, z_far_up, z_far_down, z_three_up, z_three_down, twin, other):
         pl.semaphore_signal(barrier, inc=1, device_id={"seq": peer}, device_id_type=MESH)
     for one in first_loads:
         one.wait()
-    pl.semaphore_wait(barrier, 8)
+    pl.semaphore_wait(barrier, 10)
 
     copies = Copies(send, recv)
     from_before = copies.start(bases_ref, halo.at[0], after)
@@ -189,67 +202,68 @@
 
     arrive_a, arrive_b, arrive_x, arrive_o = {}, {}, {}, {}
 
-    def send_a(src, dst, to):
-        arrive_a[dst] = copies.start(units(src, U_C, 2), units(dst, U_C, 2), to)
+    def send_a(src, dst, to, u=U_C, n=2):
+        arrive_a.setdefault(dst, []).append(copies.start(units(src, u, n), units(dst, u, n), to))
 
     def send_b(src, dst, to):
-        u, n = (U_L1, 2) if dst in NEAR else (U_L1, 1) if 0 < dst < 8 else (U_R1, 1)
-        arrive_b[dst] = copies.start(units(src, u, n), units(dst, u, n), to)
+        u, n = over_z(dst)
+        arrive_b[dst] = [copies.start(units(src, u, n), units(dst, u, n), to)] if n else []
 
     def send_x(d):
-        left, right = (U_C + 1, U_L2, 1), (U_C + 1, U_R2, 1)
-        if 0 < d < 8 and d not in NEAR:
-            right = (U_C, U_R1, 2)
-        elif d not in NEAR:
-            left = (U_C, U_L2, 2)
-        arrive_x[d] = [
-            copies.start(units(d, u, n), units(d, v, n), to)
-            for (u, v, n), to in ((left, x_up), (right, x_down))
-        ]
+        u, n = over_z(d)
+        arrive_x[d] = []
+        for side, to in ((U_L, x_up), (U_R, x_down)):
+            lacks = [i for i in (0, 1) if not u <= side + i < u + n]
+            if lacks:
+                src, dst = units(d, U_C + lacks[0], len(lacks)), units(d, side + lacks[0], len(lacks))
+                arrive_x[d].append(copies.start(src, dst, to))
 
     def send_o(d):
         if d == 0:
-            sends = ((U_L1, U_O, 1, x_up), (U_R2, U_O + 1, 1, x_down))
+            sends = ((U_L, U_O, 1, x_up), (U_R + 1, U_O + 1, 1, x_down))
         elif 0 < d < 8:
-            sends = ((U_L2, U_O, 2, x_up),)
+            sends = ((U_L, U_O, 2, x_up),)
         else:
-            sends = ((U_R1, U_O, 2, x_down),)
+            sends = ((U_R, U_O, 2, x_down),)
         arrive_o[d] = [copies.start(units(d, u, n), units(d, v, n), to) for u, v, n, to in sends]
 
-    def onward(d, send):
+    def onward(d, send, needs=lambda dst: True):
         away, back = (z_up, z_down) if d > 0 else (z_down, z_up)
         sign = 1 if d > 0 else -1
-        if abs(d) in UP:
-            send(d, sign * UP[abs(d)], away)
-        if abs(d) in BACK:
-            send(d, sign * BACK[abs(d)], back)
-        if d == (7 if send is send_a else -7):
-            send(d, 8, away)
+        following = [(sign * UP[abs(d)], away)] if abs(d) in UP else []
+        following += [(sign * BACK[abs(d)], back)] if abs(d) in BACK else []
+        for dst, to in following:
+            if needs(dst):
+                send(d, dst, to)
+        if send is send_a and d == SEED:
+            send_a(d, 8, z_three_up, U_C, 1)
+        if send is send_a and d == -SEED:
+            send_a(d, 8, z_three_down, U_C + 1, 1)
 
     send_a(0, SEED, z_far_up)
     send_a(0, -SEED, z_far_down)
-    arrive_x[0] = [
-        copies.start(units(0, u, n), units(0, v, n), to)
-        for u, v, n, to in ((U_C, U_L1, 1, x_up), (U_C, U_R1, 2, x_down), (U_C + 1, U_L2, 1, x_up))
-    ]
+    send_x(0)
     send_a(0, 1, z_up)
     send_a(0, -1, z_down)
 
     def take_a(*chunks):
         for d in chunks:
-            arrive_a[d].wait_recv()
+            for copy in arrive_a[d]:
+                copy.wait_recv()
             onward(d, send_a)
             send_x(d)
 
     def take_b(*chunks):
         for d in chunks:
-            arrive_b[d].wait_recv()
-            onward(d, send_b)
+            for copy in arrive_b.get(d, ()):
+                copy.wait_recv()
+            onward(d, send_b, lambda dst: covers(d, dst))
 
     def take_x(*chunks):
         for d in chunks:
             for copy in arrive_x[d]:
                 copy.wait_recv()
+            onward(d, send_b, lambda dst: not covers(d, dst))
             send_o(d)
 
     loads[4].wait()

time: 52.6 us -> 51 us (0.970)
  Pallas kernels: 51.8 us -> 50.2 us
    pallas_call x1, Pallas kernels: 51.8 us -> 50.2 us  [on_device(): pl.pallas_call(kernel, out_shape=jax.ShapeDtypeStruct((TOK, HEADS * VD),...]
where the time goes in v4:
time: 51 us; the launch traced here: 50.9 us
  Pallas kernels  50.2 us (98%)
  local copies, waits for them, and re-layouts  0.68 us (1%)
    pallas_call x1, Pallas kernels, on_device(): pl.pallas_call(kernel, out_shape=jax.ShapeDtypeStruct((TOK, HEADS * VD),...  50.2 us

profile of v4, /device:TPU:1, one launch (start us, length us, event | category | flops | bytes accessed | tf_op | source)
XLA Modules:
  0.0 50.9 jit_solution(15843613998535544077)
XLA Ops:
  0.0 50.2 %shard_map.109 = bf16[64,1536]{1,0:T(8,128)(2,1)S(1)} custom-call(s32[256]{0:T(256)} %bases_hbm.1, bf16[5,4,384]{2,1,0:T(4,128)(2,1)} %stem_w_hbm.1, f32[384]{0:T(512)} %stem_b_hbm.1, f32[768]{0:T(1024)} %conv_b_hbm.1, f32[768]{0:T(1024)} %gain_hbm.1, f32[64,256]{1,0:T(8,128)} %constant.4.clone.rope_hbm, f32[128,256]{1,0:T(8,128)} %constant.5.clone.step_hbm, ...), custom_call_target="tpu_custom_call" | custom-call | tf_op jit(solution)/shard_map/pallas_call | solution.py:361
  50.3 0.7 %copy.13 = bf16[64,1536]{1,0:T(8,128)(2,1)} copy(bf16[64,1536]{1,0:T(8,128)(2,1)S(1)} %shard_map.109) | data formatting | bytes 393216

commit v5 on v4

--- a/solution.py
+++ b/solution.py
@@ -284,17 +284,25 @@
 
     scale = 1.0 / math.sqrt(KD) / SOFT_CAP
     peak = SOFT_CAP * math.log2(math.e)
-    rows, width = 256, 512
-
-    def attend(tile, blocks):
-        for d in ORDER[2 * tile : 2 * tile + 2]:
-            for copy in arrive_o.pop(d, ()):
-                copy.wait_recv()
-        key_rows = buf[2 * tile : 2 * tile + 2, :, 0:32, :].reshape(width, KD)
-        value_rows = buf[2 * tile : 2 * tile + 2, :, 32:64, :].reshape(width, KD)
-        tail = buf[2 * tile : 2 * tile + 2, :, 64:80, :].reshape(width // 32, 16, KD)
+    rows = 256
+
+    def attend(chunks, first_unit, n_units, blocks):
+        if first_unit + n_units == 8:
+            for d in chunks:
+                for copy in arrive_o.pop(d, ()):
+                    copy.wait_recv()
+        start, n = ORDER.index(chunks[0]), len(chunks)
+        width = n * n_units * 32
+
+        def part_of(low, high):
+            piece = buf[start : start + n, first_unit : first_unit + n_units, low:high, :]
+            return piece.reshape(n * n_units, high - low, KD)
+
+        key_rows = part_of(0, 32).reshape(width, KD)
+        value_rows = part_of(32, 64).reshape(width, KD)
+        tail = part_of(64, 80)
         turned = pltpu.roll(tail.astype(F32).reshape(width // 2, KD), KD // 2, 1)
-        turned = turned.astype(BF16).reshape(width // 32, 16, KD)
+        turned = turned.astype(BF16).reshape(n * n_units, 16, KD)
         tail = jnp.concatenate([tail, turned], axis=1).reshape(width, KD)
         right_side = jnp.concatenate([value_rows, tail], axis=1)
         for i in blocks:
@@ -303,33 +311,35 @@
                 q_buf[at_rows, :], key_rows, (((1,), (1,)), ((), ())), preferred_element_type=F32
             )
             probability = jnp.exp2(jnp.tanh(scores * scale) * peak - peak)
-            tot[at_rows, :] += sum(probability[:, j : j + 128] for j in range(0, width, 128))
+            tot[at_rows, :] += sum(probability[:, j : j + 128] for j in range(0, width - 127, 128))
+            if width % 128:
+                tot[at_rows, : width % 128] += probability[:, width - width % 128 :]
             acc[at_rows, :] += jnp.dot(probability.astype(BF16), right_side, preferred_element_type=F32)
 
     every = range(2 * QROWS // rows)
-    tile = 0
     for k in range(1, len(STAGES) + 1):
         if k < len(STAGES):
             take_a(*STAGES[k])
         take_b(*STAGES[k - 1])
         take_x(*STAGES[k - 1])
-        known = 1 + sum(len(stage) for stage in STAGES[: k - 1])
-        while tile < min(known // 2, 7):
-            attend(tile, every)
-            tile += 1
-    while tile < 7:
-        attend(tile, every)
-        tile += 1
+        if k == 2:
+            attend((0,) + STAGES[0], 0, 8, every)
+        if k == 3:
+            attend(STAGES[1], 0, 8, every)
+            attend(STAGES[2], 0, 6, every)
+        if k == 4:
+            attend(STAGES[2], 6, 2, every)
+            attend(STAGES[3], 0, 6, every)
 
     wide = lax.broadcasted_iota(jnp.int32, (rows, 2 * KD), 1)
     home = []
     for i in (2, 3):
-        attend(7, (i,))
+        attend(STAGES[3], 6, 2, (i,))
         at_rows = pl.ds(i * rows, rows)
         total = jnp.sum(tot[at_rows, :], axis=1, keepdims=True)
         acc[at_rows, :] = jnp.where(wide < VD, acc[at_rows, :], total)
         home.append(copies.start(acc.at[at_rows], part.at[pl.ds((i - 2) * rows, rows)], twin))
-    attend(7, (0, 1))
+    attend(STAGES[3], 6, 2, (0, 1))
     for h in range(HEADS):
         if h % 4 == 0:
             home[h // 4].wait_recv()

time: 51 us -> 49.9 us (0.978)
  Pallas kernels: 50.2 us -> 49.1 us
    pallas_call x1, Pallas kernels: 50.2 us -> 49.1 us  [on_device(): pl.pallas_call(kernel, out_shape=jax.ShapeDtypeStruct((TOK, HEADS * VD),...]
where the time goes in v5:
time: 49.9 us; the launch traced here: 49.8 us
  Pallas kernels  49.1 us (98%)
  local copies, waits for them, and re-layouts  0.68 us (1%)
    pallas_call x1, Pallas kernels, on_device(): pl.pallas_call(kernel, out_shape=jax.ShapeDtypeStruct((TOK, HEADS * VD),...  49.1 us

profile of v5, /device:TPU:1, one launch (start us, length us, event | category | flops | bytes accessed | tf_op | source)
XLA Modules:
  0.0 49.8 jit_solution(9706066023519740513)
XLA Ops:
  0.0 49.1 %shard_map.109 = bf16[64,1536]{1,0:T(8,128)(2,1)S(1)} custom-call(s32[256]{0:T(256)} %bases_hbm.1, bf16[5,4,384]{2,1,0:T(4,128)(2,1)} %stem_w_hbm.1, f32[384]{0:T(512)} %stem_b_hbm.1, f32[768]{0:T(1024)} %conv_b_hbm.1, f32[768]{0:T(1024)} %gain_hbm.1, f32[64,256]{1,0:T(8,128)} %constant.4.clone.rope_hbm, f32[128,256]{1,0:T(8,128)} %constant.5.clone.step_hbm, ...), custom_call_target="tpu_custom_call" | custom-call | tf_op jit(solution)/shard_map/pallas_call | solution.py:371
  49.2 0.7 %copy.13 = bf16[64,1536]{1,0:T(8,128)(2,1)} copy(bf16[64,1536]{1,0:T(8,128)(2,1)S(1)} %shard_map.109) | data formatting | bytes 393216

commit v6 on v5

--- a/solution.py
+++ b/solution.py
@@ -110,7 +110,7 @@
     barrier = pltpu.get_barrier_semaphore()
     for peer in (x_up, x_down, z_up, z_down, z_far_up, z_far_down, z_three_up, z_three_down, twin, other):
         pl.semaphore_signal(barrier, inc=1, device_id={"seq": peer}, device_id_type=MESH)
-    for one in first_loads:
+    for one in first_loads[:2]:
         one.wait()
     pl.semaphore_wait(barrier, 10)
 
@@ -118,6 +118,8 @@
     from_before = copies.start(bases_ref, halo.at[0], after)
     from_after = copies.start(bases_ref, halo.at[1], before)
 
+    for one in first_loads[2:]:
+        one.wait()
     stem_w[...] = jnp.zeros_like(stem_w)
     for t in range(TAPS):
         stem_w[t * 8 : t * 8 + 4, :] = stem_w_ref[t].astype(F32)

time: 49.9 us -> 50 us (level)
  no operation moved by 1% of the time
where the time goes in v6:
time: 50 us; the launch traced here: 49.8 us
  Pallas kernels  49.2 us (98%)
  local copies, waits for them, and re-layouts  0.68 us (1%)
    pallas_call x1, Pallas kernels, on_device(): pl.pallas_call(kernel, out_shape=jax.ShapeDtypeStruct((TOK, HEADS * VD),...  49.2 us

profile of v6, /device:TPU:1, one launch (start us, length us, event | category | flops | bytes accessed | tf_op | source)
XLA Modules:
  0.0 49.8 jit_solution(18280797716711872471)
XLA Ops:
  0.0 49.2 %shard_map.109 = bf16[64,1536]{1,0:T(8,128)(2,1)S(1)} custom-call(s32[256]{0:T(256)} %bases_hbm.1, bf16[5,4,384]{2,1,0:T(4,128)(2,1)} %stem_w_hbm.1, f32[384]{0:T(512)} %stem_b_hbm.1, f32[768]{0:T(1024)} %conv_b_hbm.1, f32[768]{0:T(1024)} %gain_hbm.1, f32[64,256]{1,0:T(8,128)} %constant.4.clone.rope_hbm, f32[128,256]{1,0:T(8,128)} %constant.5.clone.step_hbm, ...), custom_call_target="tpu_custom_call" | custom-call | tf_op jit(solution)/shard_map/pallas_call | solution.py:373
  49.2 0.7 %copy.13 = bf16[64,1536]{1,0:T(8,128)(2,1)} copy(bf16[64,1536]{1,0:T(8,128)(2,1)S(1)} %shard_map.109) | data formatting | bytes 393216
